TPU v7x, 32 devices: a whole 2x2x4 slice. The times are simulated.
32 devices in a mesh: parts: 2 (over y), row: 4 (over z), col: 4 (over x, core).
Axes of the slice: x: 2, y: 2, z: 4, core: 2. Of those that a mesh axis runs over, the one named last changes fastest.
Arguments:
- single: bfloat16 [8, 1024, 768], P(None, ('parts', 'row'), 'col'), parts along dimension 1, may hold values from -6 to 6
- pair_act: bfloat16 [1024, 512, 128], P(('parts', 'row'), 'col'), parts along dimension 0, may hold values from -6 to 6
- token_mask: int32 [1024], P(('parts', 'row')), parts along dimension 0, may hold values 0 or 1
- atom_feats: bfloat16 [8192, 128], P(('parts', 'row', 'col')), parts along dimension 0, may hold values from -6 to 6
- atom_token: int32 [8192], P(('parts', 'row', 'col')), parts along dimension 0, may hold values from 0 to 127, as said below
- atom_count: int32 [32], P(('parts', 'row', 'col')), parts along dimension 0, may hold values from 32 to 256, as said below
- atom_weight: bfloat16 [128, 768], P(None, 'col'), may hold values from -0.5 to 0.5
- bias_weight: bfloat16 [128, 2, 16], replicated, may hold values from -16 to 16
- qkvg_weight: bfloat16 [2, 4, 768, 768], P(None, None, 'col'), may hold values from -0.21875 to 0.21875
- out_weight: bfloat16 [2, 768, 768], P(None, 'col'), may hold values from -0.21875 to 0.21875
Outputs:
- updated: bfloat16 [8, 1024, 768], P(None, ('parts', 'row'), 'col'), parts along dimension 1
There are 2 independent parts, one for each index of `parts`. A program takes and returns all parts, laid end to end along the dimension named above; an argument that names none is the same for every part. Nothing has to cross between parts.
Inputs may be any that keep to these rules, and one draw needn't show every extreme that they name: `atom_token`: slots of a device hold atoms of the 128 tokens of that device's row block, numbered within the block; every token owns at least one live slot. The first atom_count slots of a device are live, the others are padding; in every draw some device has all 256 slots live.
All inputs are finite; a program needn't handle non-finite values. No bound on the sum of `token_mask` on one device may be relied on, other than what follows from the above.
Results may differ from a plain program's by a relative error of at most 0.014.
The roundings to bfloat16 on the way count: a program that leaves them out, or rounds other values in their place, can miss the bound.
Values may be sent and summed in bfloat16 or wider, within the bound.
A program may use at most 64 MiB of HBM per device.

v0:
```python
import math
import jax
import jax.numpy as jnp
from jax import lax
from jax.sharding import PartitionSpec as P

HEAD_DIM = 48
LAYERS = 2
EPS = 1e-05
MASKED = -1000000000.0
START_LOW = -1e30


def layer_norm(values):
    average = jnp.mean(values, axis=-1, keepdims=True)
    centered = values - average
    variance = jnp.mean(centered * centered, axis=-1, keepdims=True)
    return centered * lax.rsqrt(variance + EPS)


def per_device(
    single,
    pair_act,
    token_mask,
    atom_feats,
    atom_token,
    atom_count,
    atom_weight,
    bias_weight,
    qkvg_weight,
    out_weight,
):
    tok_rows = single.shape[1]
    sample_count = single.shape[0]
    slot_ids = jnp.arange(atom_feats.shape[0], dtype=jnp.int32)
    live_slots = slot_ids < atom_count[0]
    token_ids = jnp.arange(tok_rows, dtype=jnp.int32)
    owner_match = (token_ids[:, None] == atom_token[None, :]) & live_slots[None, :]
    owners = owner_match.astype(jnp.float32)
    counts = jnp.sum(owners, axis=1)
    atom_sums = jnp.dot(
        owner_match.astype(jnp.bfloat16), atom_feats, preferred_element_type=jnp.float32
    )
    sum_total, count_total = (
        lax.psum(atom_sums.astype(jnp.bfloat16), "col").astype(jnp.float32),
        lax.psum(counts[:, None].astype(jnp.bfloat16), "col").astype(jnp.float32),
    )
    pooled = (
        jnp.dot(sum_total, atom_weight.astype(jnp.float32), precision=lax.Precision.HIGHEST)
        / count_total
    )
    stream = (single.astype(jnp.float32) + pooled[None]).astype(jnp.bfloat16)
    pair_normed = layer_norm(pair_act.astype(jnp.float32)).astype(jnp.bfloat16)
    biases = jnp.einsum(
        "ijc,clh->lhij", pair_normed, bias_weight, preferred_element_type=jnp.float32
    ).astype(jnp.bfloat16)
    live_keys = (token_mask > 0).astype(jnp.bfloat16)[None, :]
    score_scale = 1.0 / math.sqrt(HEAD_DIM)
    for layer_idx in range(LAYERS):
        spread = lax.all_to_all(biases[layer_idx], "col", split_axis=0, concat_axis=2, tiled=True)
        gathered = lax.all_gather(stream, "col", axis=2, tiled=True)
        normed = layer_norm(gathered.astype(jnp.float32)).astype(jnp.bfloat16)
        projected = jnp.einsum(
            "std,fed->fste", normed, qkvg_weight[layer_idx], preferred_element_type=jnp.float32
        )
        head_width = projected.shape[3]
        heads_here = head_width // HEAD_DIM
        queries = (
            projected[0].astype(jnp.bfloat16).reshape(sample_count, tok_rows, heads_here, HEAD_DIM)
        )
        key_rows = projected[1].astype(jnp.bfloat16)
        value_rows = projected[2].astype(jnp.bfloat16)
        gating = jax.nn.sigmoid(projected[3])

        def attend(running, incoming, offset, queries=queries, spread=spread):
            top_old, summed_old, acc_old = running
            keys_in, values_in, live_in = incoming
            key_count = keys_in.shape[1]
            keys_heads = keys_in.reshape(sample_count, key_count, heads_here, HEAD_DIM)
            values_heads = values_in.reshape(sample_count, key_count, heads_here, HEAD_DIM)
            scores = (
                jnp.einsum(
                    "sqhd,skhd->shqk", queries, keys_heads, preferred_element_type=jnp.float32
                )
                * score_scale
            )
            scores = scores + spread.astype(jnp.float32)[None]
            scores = jnp.where(live_in[0][None, None, None, :] > 0, scores, MASKED)
            top_new = jnp.maximum(top_old, jnp.max(scores, axis=-1))
            exponent = jnp.exp(scores - top_new[..., None])
            summed_new = jnp.sum(exponent, axis=-1)
            weights = exponent.astype(jnp.bfloat16)
            acc_new = jnp.einsum(
                "shqk,skhd->shqd", weights, values_heads, preferred_element_type=jnp.float32
            )
            return (top_new, summed_new, acc_new)

        start_state = (
            jnp.full((sample_count, heads_here, tok_rows), START_LOW, jnp.float32),
            jnp.zeros((sample_count, heads_here, tok_rows), jnp.float32),
            jnp.zeros((sample_count, heads_here, tok_rows, HEAD_DIM), jnp.float32),
        )
        top_end, summed_end, acc_end = attend(
            start_state,
            (
                lax.all_gather(key_rows, "row", axis=1, tiled=True),
                lax.all_gather(value_rows, "row", axis=1, tiled=True),
                lax.all_gather(live_keys, "row", axis=1, tiled=True),
            ),
            jnp.int32(0),
        )
        attended = acc_end / summed_end[..., None]
        attended = attended.transpose(0, 2, 1, 3).reshape(sample_count, tok_rows, head_width)
        gated = (gating * attended).astype(jnp.bfloat16)
        out_rows = out_weight[layer_idx]

        def project(summed, incoming, offset, out_rows=out_rows):
            return jnp.einsum("std,ed->ste", incoming, out_rows, preferred_element_type=jnp.float32)

        zero_update = jnp.zeros((sample_count, tok_rows, out_rows.shape[0]), jnp.float32)
        update = project(
            zero_update, lax.all_gather(gated, "col", axis=2, tiled=True), jnp.int32(0)
        )
        stream = (stream.astype(jnp.float32) + update).astype(jnp.bfloat16)
    return stream


def solution(mesh):
    placed = (
        P(None, ("parts", "row"), "col"),
        P(("parts", "row"), "col", None),
        P(("parts", "row")),
        P(("parts", "row", "col"), None),
        P(("parts", "row", "col")),
        P(("parts", "row", "col")),
        P(None, "col"),
        P(),
        P(None, None, "col", None),
        P(None, "col", None),
    )
    return jax.shard_map(
        per_device,
        mesh=mesh,
        in_specs=placed,
        out_specs=P(None, ("parts", "row"), "col"),
        check_vma=False,
    )
```

profile of v0, /device:TPU:0, one launch (start us, length us, event | category | flops | bytes accessed | tf_op | source)
XLA Modules:
  0.0 297.7 jit_solution(7858886814213033118)
XLA Ops:
  7.4 0.8 convert_reduce_fusion.3
  8.2 0.0 copy-done
  8.2 0.8 convolution_convert_fusion
  9.0 13.2 %all-reduce = (bf16[128,128]{1,0:T(8,128)(2,1)S(1)}, bf16[128]{0:T(256)(128)(2,1)S(1)}) all-reduce(bf16[128,128]{1,0:T(8,128)(2,1)S(1)} %convolution_convert_fusion, bf16[128]{0:T(256)(128)(2,1)S(1)} %convert_reduce_fusion.3), channel_id=1, replica_groups=mesh['parts'=2,'row'=4,'col'=4] {'col'}, use_global_device_ids=true, to_apply=%region_0.0 | all-reduce | flops 16512 | bytes 66048 | tf_op jit(solution)/shard_map/psum | solution.py:45
  22.2 1.0 convolution_divide_fusion
  23.1 1.8 add_convert_fusion
  25.0 0.0 all-gather.15.cloned.1.call-update
  25.0 0.0 all-gather.23.cloned.1.call-start
  25.0 20.1 %all-gather.15.cloned.1.call-done = bf16[8,128,768]{1,2,0:T(8,128)(2,1)} async-done(((bf16[8,128,192]{1,2,0:T(8,128)(2,1)}), bf16[8,128,768]{1,2,0:T(8,128)(2,1)}) %all-gather.15.cloned.1.call-update) | async-done | bytes 1572880 | tf_op jit(solution)/shard_map/all_gather | solution.py:61
  45.1 1.7 convert_reduce_fusion.2
  46.8 1.8 fusion.25
  48.7 3.2 %fusion.87 = (bf16[4,8,128,192]{2,3,0,1:T(8,128)(2,1)S(1)}, f32[4,8,128,192]{2,3,0,1:T(8,128)}) fusion(bf16[2,4,192,768]{3,2,1,0:T(8,128)(2,1)S(1)} %copy-done.9, bf16[8,128,768]{1,2,0:T(8,128)(2,1)S(1)} %copy-done.4, f32[8,128]{1,0:T(8,128)S(1)} %add_rsqrt_fusion.2, f32[8,128]{1,0:T(8,128)S(1)} %broadcast_multiply_fusion.2), kind=kOutput, calls=%fused_computation.107 | convolution fusion | flops 1211891712 | bytes 7479296 | tf_op jit(solution)/shard_map/std,fed->fste/dot_general | solution.py:63
  51.9 1.0 fusion.86
  52.9 0.0 all-gather.23.cloned.1.call-update
  52.9 0.0 all-gather.25.cloned.1.call-start
  53.0 0.0 copy-start.3
  53.0 3.5 %convert_reduce_fusion = f32[128,128]{1,0:T(8,128)S(1)} fusion(bf16[128,128,128]{2,1,0:T(8,128)(2,1)} %param.11), kind=kLoop, calls=%fused_computation.1 | loop fusion | flops 4177920 | bytes 4259840 | tf_op jit(solution)/shard_map/reduce_sum | solution.py:15
  56.5 0.0 copy-start.10
  56.5 4.8 %fusion.2 = f32[128,128]{1,0:T(8,128)S(1)} fusion(bf16[128,128,128]{2,1,0:T(8,128)(2,1)S(1)} %copy-done.3, f32[128,128]{1,0:T(8,128)S(1)} %broadcast_multiply_fusion), kind=kLoop, calls=%fused_computation.4 | loop fusion | flops 8372224 | bytes 4325376 | tf_op jit(solution)/shard_map/reduce_sum | solution.py:17
  61.4 6.0 %fusion.38 = bf16[2,16,128,128]{3,1,0,2:T(8,128)(2,1)S(1)} fusion(bf16[128,128,128]{2,1,0:T(8,128)(2,1)S(1)} %copy-done.3, f32[128,128]{1,0:T(8,128)S(1)} %add_rsqrt_fusion, f32[128,128]{1,0:T(8,128)S(1)} %broadcast_multiply_fusion, bf16[128,2,16]{0,2,1:T(8,128)(2,1)S(1)} %copy-done.10), kind=kOutput, calls=%fused_computation.43 | convolution fusion | flops 143130624 | bytes 5382144 | tf_op jit(solution)/shard_map/ijc,clh->lhij/dot_general | solution.py:54
  67.3 0.0 copy-start.11
  67.3 0.0 all-gather.25.cloned.1.call-update
  67.4 0.2 slice_bitcast_fusion
  67.6 0.9 copy.26
  68.5 3.5 %all-to-all-start = ((bf16[16,128,128]{2,1,0:T(8,128)(2,1)}), bf16[16,128,128]{2,1,0:T(8,128)(2,1)S(1)}, u32[]{:S(2)}, u32[]{:S(2)}) async-start(bf16[16,128,128]{2,1,0:T(8,128)(2,1)} %copy.26), calls=%async_computation | async-start | bytes 1048576 | tf_op jit(solution)/shard_map/all_to_all | solution.py:60
  72.0 0.0 all-gather.17.cloned.1.call-start
  72.0 12.2 %all-gather.5 = bf16[4,1,128]{2,1,0:T(2,128)(2,1)S(1)} all-gather(bf16[1,1,128]{2,1,0:T(2,128)(2,1)S(1)} %fusion.80), channel_id=2, replica_groups=mesh['parts'=2,'row'=4,'col'=4] {'row'}, dimensions={0}, use_global_device_ids=true | all-gather | bytes 1280 | tf_op jit(solution)/shard_map/all_gather | solution.py:108
  84.3 0.0 all-to-all-done
  84.3 0.1 copy_bitcast_fusion.1
  84.4 6.4 %all-gather.23.cloned.1.call-done = bf16[1,8,512,192]{2,3,0,1:T(8,128)(2,1)} async-done(((bf16[1,8,128,192]{2,3,0,1:T(8,128)(2,1)}), bf16[1,8,512,192]{2,3,0,1:T(8,128)(2,1)}) %all-gather.23.cloned.1.call-update) | async-done | bytes 1572880 | tf_op jit(solution)/shard_map/all_gather | solution.py:106
  90.8 3.3 %fusion.8 = (f32[8,4,128]{2,1,0:T(4,128)S(1)}, f32[8,4,128,512]{3,2,1,0:T(8,128)S(1)}) fusion(f32[4,128,512]{2,1,0:T(8,128)S(1)} %copy_bitcast_fusion.1, pred[512]{0:T(512)(128)(4,1)S(1)} %bitcast.132, bf16[8,128,4,48]{1,3,2,0:T(8,128)(2,1)S(1)} %bitcast.126, bf16[8,512,4,48]{1,3,2,0:T(8,128)(2,1)} %bitcast.128), kind=kOutput, calls=%fused_computation.14 | convolution fusion | flops 209711104 | bytes 11420160 | tf_op jit(solution)/shard_map/sqhd,skhd->shqk/dot_general | solution.py:82
  94.1 3.2 %copy-done.2 = f32[8,4,128,512]{3,2,1,0:T(8,128)} copy-done((f32[8,4,128,512]{3,2,1,0:T(8,128)}, f32[8,4,128,512]{3,2,1,0:T(8,128)S(1)}, u32[]{:S(2)}) %copy-start.2) | copy-done | bytes 8388632
  97.3 2.3 fusion.4
  99.7 28.6 %all-gather.25.cloned.1.call-done = bf16[1,8,512,192]{2,3,0,1:T(8,128)(2,1)} async-done(((bf16[1,8,128,192]{2,3,0,1:T(8,128)(2,1)}), bf16[1,8,512,192]{2,3,0,1:T(8,128)(2,1)}) %all-gather.25.cloned.1.call-update) | async-done | bytes 1572880 | tf_op jit(solution)/shard_map/all_gather | solution.py:107
  128.3 6.3 %fusion.56 = f32[8,128,4,48]{1,3,2,0:T(8,128)S(1)} fusion(bf16[8,512,4,48]{1,3,2,0:T(8,128)(2,1)} %bitcast.138, f32[8,4,128,512]{3,2,1,0:T(8,128)} %copy-done.2, f32[8,4,128]{2,1,0:T(4,128)S(1)} %broadcast_maximum_fusion.1, f32[4,128,512]{2,1,0:T(8,128)S(1)} %copy_bitcast_fusion.1, pred[512]{0:T(512)(128)(4,1)S(1)} %bitcast.134, f32[8,128,4]{1,2,0:T(4,128)S(1)} %bitcast.131), kind=kOutput, calls=%fused_computation.61 | convolution fusion | flops 212008960 | bytes 11829760 | tf_op jit(solution)/shard_map/shqk,skhd->shqd/dot_general | solution.py:93
  134.6 2.2 fusion.69
  136.8 0.0 all-gather.17.cloned.1.call-update
  136.8 0.0 all-gather.19.cloned.1.call-start
  136.8 18.0 %all-gather.17.cloned.1.call-done = bf16[8,128,768]{1,2,0:T(8,128)(2,1)} async-done(((bf16[8,128,192]{1,2,0:T(8,128)(2,1)}), bf16[8,128,768]{1,2,0:T(8,128)(2,1)}) %all-gather.17.cloned.1.call-update) | async-done | bytes 1572880 | tf_op jit(solution)/shard_map/all_gather | solution.py:122
  154.8 2.6 fusion.47
  157.4 0.0 all-gather.19.cloned.1.call-update
  157.5 0.0 all-gather.27.cloned.1.call-start
  157.5 19.7 %all-gather.19.cloned.1.call-done = bf16[8,128,768]{1,2,0:T(8,128)(2,1)} async-done(((bf16[8,128,192]{1,2,0:T(8,128)(2,1)}), bf16[8,128,768]{1,2,0:T(8,128)(2,1)}) %all-gather.19.cloned.1.call-update) | async-done | bytes 1572880 | tf_op jit(solution)/shard_map/all_gather | solution.py:61
  177.3 1.7 convert_reduce_fusion.1
  179.0 1.8 fusion.23
  180.9 4.5 %fusion.88 = (bf16[4,8,128,192]{2,3,0,1:T(8,128)(2,1)S(1)}, f32[4,8,128,192]{2,3,0,1:T(8,128)}) fusion(bf16[2,4,192,768]{3,2,1,0:T(8,128)(2,1)} %param.18, bf16[8,128,768]{1,2,0:T(8,128)(2,1)S(1)} %copy-done.5, f32[8,128]{1,0:T(8,128)S(1)} %add_rsqrt_fusion.1, f32[8,128]{1,0:T(8,128)S(1)} %broadcast_multiply_fusion.1), kind=kOutput, calls=%fused_computation.108 | convolution fusion | flops 1211891712 | bytes 7479296 | tf_op jit(solution)/shard_map/std,fed->fste/dot_general | solution.py:63
  185.3 1.0 fusion.85
  186.3 0.0 all-gather.27.cloned.1.call-update
  186.4 0.0 all-gather.29.cloned.1.call-start
  186.4 0.7 all-gather.29.cloned.1.call-update
  187.1 0.0 all-gather.21.cloned.1.call-start
  187.2 0.1 copy.29
  187.3 11.2 %all_to_all.8 = bf16[16,128,128]{2,1,0:T(8,128)(2,1)S(1)} all-to-all(bf16[16,128,128]{2,1,0:T(8,128)(2,1)S(1)} %copy.29), channel_id=1, replica_groups=mesh['parts'=2,'row'=4,'col'=4] {'col'}, dimensions={0} | all-to-all | bytes 1048576 | tf_op jit(solution)/shard_map/all_to_all | solution.py:60
  198.5 0.1 copy_bitcast_fusion
  198.7 25.6 %all-gather.27.cloned.1.call-done = bf16[1,8,512,192]{2,3,0,1:T(8,128)(2,1)} async-done(((bf16[1,8,128,192]{2,3,0,1:T(8,128)(2,1)}), bf16[1,8,512,192]{2,3,0,1:T(8,128)(2,1)}) %all-gather.27.cloned.1.call-update) | async-done | bytes 1572880 | tf_op jit(solution)/shard_map/all_gather | solution.py:106
  224.2 3.3 %fusion.9 = (f32[8,4,128]{2,1,0:T(4,128)S(1)}, f32[8,4,128,512]{3,2,1,0:T(8,128)S(1)}) fusion(f32[4,128,512]{2,1,0:T(8,128)S(1)} %copy_bitcast_fusion, pred[512]{0:T(512)(128)(4,1)S(1)} %bitcast.135, bf16[8,128,4,48]{1,3,2,0:T(8,128)(2,1)S(1)} %bitcast.127, bf16[8,512,4,48]{1,3,2,0:T(8,128)(2,1)} %bitcast.129), kind=kOutput, calls=%fused_computation.15 | convolution fusion | flops 209711104 | bytes 11420160 | tf_op jit(solution)/shard_map/sqhd,skhd->shqk/dot_general | solution.py:82
  227.5 3.2 %copy-done.1 = f32[8,4,128,512]{3,2,1,0:T(8,128)} copy-done((f32[8,4,128,512]{3,2,1,0:T(8,128)}, f32[8,4,128,512]{3,2,1,0:T(8,128)S(1)}, u32[]{:S(2)}) %copy-start.1) | copy-done | bytes 8388632
  230.7 2.3 fusion.6
  233.1 28.6 %all-gather.29.cloned.1.call-done = bf16[1,8,512,192]{2,3,0,1:T(8,128)(2,1)} async-done(((bf16[1,8,128,192]{2,3,0,1:T(8,128)(2,1)}), bf16[1,8,512,192]{2,3,0,1:T(8,128)(2,1)}) %all-gather.29.cloned.1.call-update) | async-done | bytes 1572880 | tf_op jit(solution)/shard_map/all_gather | solution.py:107
  261.7 6.3 %fusion.53 = f32[8,128,4,48]{1,3,2,0:T(8,128)S(1)} fusion(bf16[8,512,4,48]{1,3,2,0:T(8,128)(2,1)} %bitcast.139, f32[8,4,128,512]{3,2,1,0:T(8,128)} %copy-done.1, f32[8,4,128]{2,1,0:T(4,128)S(1)} %broadcast_maximum_fusion, f32[4,128,512]{2,1,0:T(8,128)S(1)} %copy_bitcast_fusion, pred[512]{0:T(512)(128)(4,1)S(1)} %bitcast.137, f32[8,128,4]{1,2,0:T(4,128)S(1)} %bitcast.130), kind=kOutput, calls=%fused_computation.60 | convolution fusion | flops 212008960 | bytes 11829760 | tf_op jit(solution)/shard_map/shqk,skhd->shqd/dot_general | solution.py:93
  268.0 2.2 fusion.70
  270.2 0.0 all-gather.21.cloned.1.call-update
  270.2 18.0 %all-gather.21.cloned.1.call-done = bf16[8,128,768]{1,2,0:T(8,128)(2,1)} async-done(((bf16[8,128,192]{1,2,0:T(8,128)(2,1)}), bf16[8,128,768]{1,2,0:T(8,128)(2,1)}) %all-gather.21.cloned.1.call-update) | async-done | bytes 1572880 | tf_op jit(solution)/shard_map/all_gather | solution.py:122
  288.2 2.6 fusion.48
  (31 shorter events, 0.1 us)
Async XLA Ops:
  6.5 1.6 copy-start
  6.5 42.2 %copy-start.9 = (bf16[2,4,192,768]{3,2,1,0:T(8,128)(2,1)S(1)}, bf16[2,4,192,768]{3,2,1,0:T(8,128)(2,1)}, u32[]{:S(2)}) copy-start(bf16[2,4,192,768]{3,2,1,0:T(8,128)(2,1)} %param.18) | copy-start | bytes 7077892
  6.5 38.6 %all-gather.15.cloned.1.call-start = ((), (), s32[]{:S(2)}) async-start(), calls=%async_computation.2 | async-start | bytes 1966080 | tf_op jit(solution)/shard_map/all_gather | solution.py:61
  25.0 65.8 %all-gather.23.cloned.1.call-start = ((), (), s32[]{:S(2)}) async-start(), calls=%async_computation.6 | async-start | bytes 1966080 | tf_op jit(solution)/shard_map/all_gather | solution.py:106
  45.1 3.6 %copy-start.4 = (bf16[8,128,768]{1,2,0:T(8,128)(2,1)S(1)}, bf16[8,128,768]{1,2,0:T(8,128)(2,1)}, u32[]{:S(2)}) copy-start(bf16[8,128,768]{1,2,0:T(8,128)(2,1)} %all-gather.15.cloned.1.call-done) | copy-start | bytes 4718596
  52.9 75.3 %all-gather.25.cloned.1.call-start = ((), (), s32[]{:S(2)}) async-start(), calls=%async_computation.7 | async-start | bytes 1966080 | tf_op jit(solution)/shard_map/all_gather | solution.py:107
  53.0 3.6 %copy-start.3 = (bf16[128,128,128]{2,1,0:T(8,128)(2,1)S(1)}, bf16[128,128,128]{2,1,0:T(8,128)(2,1)}, u32[]{:S(2)}) copy-start(bf16[128,128,128]{2,1,0:T(8,128)(2,1)} %param.11) | copy-start | bytes 12582916
  56.5 4.8 %copy-start.10 = (bf16[128,2,16]{0,2,1:T(8,128)(2,1)S(1)}, bf16[128,2,16]{0,2,1:T(8,128)(2,1)}, u32[]{:S(2)}) copy-start(bf16[128,2,16]{0,2,1:T(8,128)(2,1)} %param.17) | copy-start | bytes 24580
  67.3 4.7 %copy-start.11 = (s32[128]{0:T(128)S(1)}, s32[128]{0:T(128)}, u32[]{:S(2)}) copy-start(s32[128]{0:T(128)} %param.12) | copy-start | bytes 1540
  68.5 15.8 %all-to-all-start = ((bf16[16,128,128]{2,1,0:T(8,128)(2,1)}), bf16[16,128,128]{2,1,0:T(8,128)(2,1)S(1)}, u32[]{:S(2)}, u32[]{:S(2)}) async-start(bf16[16,128,128]{2,1,0:T(8,128)(2,1)} %copy.26), calls=%async_computation | async-start | bytes 1048576 | tf_op jit(solution)/shard_map/all_to_all | solution.py:60
  72.0 82.8 %all-gather.17.cloned.1.call-start = ((), (), s32[]{:S(2)}) async-start(), calls=%async_computation.3 | async-start | bytes 1966080 | tf_op jit(solution)/shard_map/all_gather | solution.py:122
  94.1 3.2 %copy-start.2 = (f32[8,4,128,512]{3,2,1,0:T(8,128)}, f32[8,4,128,512]{3,2,1,0:T(8,128)S(1)}, u32[]{:S(2)}) copy-start(f32[8,4,128,512]{3,2,1,0:T(8,128)S(1)} %get-tuple-element.18) | copy-start | bytes 25165828
  128.3 26.5 %copy-start.6 = (bf16[8,128,192]{1,2,0:T(8,128)(2,1)S(1)}, bf16[8,128,192]{1,2,0:T(8,128)(2,1)}, u32[]{:S(2)}) copy-start(bf16[8,128,192]{1,2,0:T(8,128)(2,1)} %add_convert_fusion) | copy-start | bytes 1179652
  128.3 26.5 %copy-start.8 = (bf16[2,192,768]{2,1,0:T(8,128)(2,1)S(1)}, bf16[2,192,768]{2,1,0:T(8,128)(2,1)}, u32[]{:S(2)}) copy-start(bf16[2,192,768]{2,1,0:T(8,128)(2,1)} %param.19) | copy-start | bytes 1769476
  136.8 40.5 %all-gather.19.cloned.1.call-start = ((), (), s32[]{:S(2)}) async-start(), calls=%async_computation.4 | async-start | bytes 1966080 | tf_op jit(solution)/shard_map/all_gather | solution.py:61
  157.5 66.7 %all-gather.27.cloned.1.call-start = ((), (), s32[]{:S(2)}) async-start(), calls=%async_computation.8 | async-start | bytes 1966080 | tf_op jit(solution)/shard_map/all_gather | solution.py:106
  177.3 3.6 %copy-start.5 = (bf16[8,128,768]{1,2,0:T(8,128)(2,1)S(1)}, bf16[8,128,768]{1,2,0:T(8,128)(2,1)}, u32[]{:S(2)}) copy-start(bf16[8,128,768]{1,2,0:T(8,128)(2,1)} %all-gather.19.cloned.1.call-done) | copy-start | bytes 4718596
  186.4 75.3 %all-gather.29.cloned.1.call-start = ((), (), s32[]{:S(2)}) async-start(), calls=%async_computation.9 | async-start | bytes 1966080 | tf_op jit(solution)/shard_map/all_gather | solution.py:107
  187.1 101.1 %all-gather.21.cloned.1.call-start = ((), (), s32[]{:S(2)}) async-start(), calls=%async_computation.5 | async-start | bytes 1966080 | tf_op jit(solution)/shard_map/all_gather | solution.py:122
  227.5 3.2 %copy-start.1 = (f32[8,4,128,512]{3,2,1,0:T(8,128)}, f32[8,4,128,512]{3,2,1,0:T(8,128)S(1)}, u32[]{:S(2)}) copy-start(f32[8,4,128,512]{3,2,1,0:T(8,128)S(1)} %get-tuple-element.22) | copy-start | bytes 25165828
  261.7 26.5 %copy-start.7 = (bf16[8,128,192]{1,2,0:T(8,128)(2,1)S(1)}, bf16[8,128,192]{1,2,0:T(8,128)(2,1)}, u32[]{:S(2)}) copy-start(bf16[8,128,192]{1,2,0:T(8,128)(2,1)} %fusion.47) | copy-start | bytes 1179652
Sparse Core Ops, SparseCore 0:
  25.1 19.9 all-gather.14
  53.0 37.7 all-gather.22
  92.4 35.8 all-gather.24
  136.9 17.8 all-gather.16
  157.6 19.6 all-gather.18
  186.5 37.6 all-gather.26
  225.8 35.9 all-gather.28
  270.3 17.8 all-gather.20
where the time goes:
time: 298 us
  waiting for transfers between devices  166 us (56%)
  matrix products  39.9 us (13%)
  blocking collectives  36.6 us (12%)
  other arithmetic  27.3 us (9%)
  between operations  14.6 us (5%)
  local copies, waits for them, and re-layouts  9.73 us (3%)
  starting transfers between devices  3.76 us (1%)
    all_gather x2, waiting for transfers between devices, per_device(): lax.all_gather(value_rows, 'row', axis=1, tiled=True)  57.2 us
    all_gather x2, waiting for transfers between devices, per_device(): gathered = lax.all_gather(stream, 'col', axis=2, tiled=True)  39.8 us
    all_gather x2, waiting for transfers between devices, per_device(): lax.all_gather(gated, 'col', axis=2, tiled=True)  36 us
    all_gather x2, waiting for transfers between devices, per_device(): lax.all_gather(key_rows, 'row', axis=1, tiled=True)  31.9 us
    psum x1, blocking collectives, per_device(): lax.psum(atom_sums.astype(jnp.bfloat16), 'col').astype(jnp.float32)  13.2 us
    dot_general x2, matrix products, attend(): jnp.einsum('shqk,skhd->shqd', weights, values_heads, preferred_element_ty...  12.6 us
    all_gather x1, blocking collectives, per_device(): lax.all_gather(live_keys, 'row', axis=1, tiled=True)  12.2 us
    all_to_all x1, blocking collectives, per_device(): lax.all_to_all(biases[layer_idx], 'col', split_axis=0, concat_axis=2, til...  11.2 us
  transfers between devices with their start and end apart: 9, of which 8 were waited for; matrix products, arithmetic and copies ran while one was open for 9% of the time, Pallas kernels for 0%

commit v1 on v0

--- a/solution.py
+++ b/solution.py
@@ -9,6 +9,18 @@
 EPS = 1e-05
 MASKED = -1000000000.0
 START_LOW = -1e30
+
+
+def collect(value, axis, dim):
+    ways, here, lap = (lax.axis_size(axis), lax.axis_index(axis), value.shape[dim])
+    shape = [n * ways if d == dim else n for d, n in enumerate(value.shape)]
+    full = lax.dynamic_update_slice_in_dim(
+        jnp.zeros(shape, value.dtype), value, here * lap, axis=dim
+    )
+    for far in range(1, ways):
+        value = lax.ppermute(value, axis, [(d, (d + 1) % ways) for d in range(ways)])
+        full = lax.dynamic_update_slice_in_dim(full, value, (here - far) % ways * lap, axis=dim)
+    return full
 
 
 def layer_norm(values):
@@ -103,7 +115,7 @@
         top_end, summed_end, acc_end = attend(
             start_state,
             (
-                lax.all_gather(key_rows, "row", axis=1, tiled=True),
+                collect(key_rows, "row", 1),
                 lax.all_gather(value_rows, "row", axis=1, tiled=True),
                 lax.all_gather(live_keys, "row", axis=1, tiled=True),
             ),

time: 298 us -> 274 us (0.919)
  waiting for transfers between devices: 166 us -> 140 us
  blocking collectives: 36.6 us -> 27.9 us
  starting transfers between devices: 3.76 us -> 11.6 us
  local copies, waits for them, and re-layouts: 9.73 us -> 14.6 us
    ppermute x0 -> x6, waiting for transfers between devices: none -> 49.5 us  [collect(): lax.ppermute(value, axis, [(d, (d + 1) % ways) for d in range(ways)])]
    all_gather x2, waiting for transfers between devices: 57.2 us -> 21.6 us  [per_device(): lax.all_gather(value_rows, 'row', axis=1, tiled=True)]
    all_gather x2 -> x0, waiting for transfers between devices: 31.9 us -> none  [per_device(): lax.all_gather(key_rows, 'row', axis=1, tiled=True)]
    all_to_all x1 -> x0, blocking collectives: 11.2 us -> none  [per_device(): lax.all_to_all(biases[layer_idx], 'col', split_axis=0, concat_axis=2, til...]
    all_gather x2, waiting for transfers between devices: 39.8 us -> 31.5 us  [per_device(): gathered = lax.all_gather(stream, 'col', axis=2, tiled=True)]
    ppermute x0 -> x6, starting transfers between devices: none -> 4.47 us  [collect(): lax.ppermute(value, axis, [(d, (d + 1) % ways) for d in range(ways)])]
    all_to_all x1 -> x2, starting transfers between devices: 3.47 us -> 6.94 us  [per_device(): lax.all_to_all(biases[layer_idx], 'col', split_axis=0, concat_axis=2, til...]
    unnamed x24 -> x30, local copies, waits for them, and re-layouts: 6.48 us -> 7.62 us
  transfers between devices with their start and end apart: 9 -> 14, of which waited for: 8 -> 12; matrix products, arithmetic and copies ran while one was open for 9% -> 10% of each run, Pallas kernels for 0% -> 0%
where the time goes in v1:
time: 274 us
  waiting for transfers between devices  140 us (51%)
  matrix products  37.1 us (14%)
  blocking collectives  27.9 us (10%)
  other arithmetic  27.3 us (10%)
  local copies, waits for them, and re-layouts  14.6 us (5%)
  between operations  14.6 us (5%)
  starting transfers between devices  11.6 us (4%)
    ppermute x6, waiting for transfers between devices, collect(): lax.ppermute(value, axis, [(d, (d + 1) % ways) for d in range(ways)])  49.5 us
    all_gather x2, waiting for transfers between devices, per_device(): lax.all_gather(gated, 'col', axis=2, tiled=True)  36.1 us
    all_gather x2, waiting for transfers between devices, per_device(): gathered = lax.all_gather(stream, 'col', axis=2, tiled=True)  31.5 us
    all_gather x2, waiting for transfers between devices, per_device(): lax.all_gather(value_rows, 'row', axis=1, tiled=True)  21.6 us
    all_gather x1, blocking collectives, per_device(): lax.all_gather(live_keys, 'row', axis=1, tiled=True)  14.7 us
    psum x1, blocking collectives, per_device(): lax.psum(atom_sums.astype(jnp.bfloat16), 'col').astype(jnp.float32)  13.2 us
    dot_general x2, matrix products, attend(): jnp.einsum('shqk,skhd->shqd', weights, values_heads, preferred_element_ty...  12.6 us
    reduce_sum x3, other arithmetic, layer_norm(): variance = jnp.mean(centered * centered, axis=-1, keepdims=True)  8.43 us
  transfers between devices with their start and end apart: 14, of which 12 were waited for; matrix products, arithmetic and copies ran while one was open for 10% of the time, Pallas kernels for 0%

profile of v1, /device:TPU:0, one launch (start us, length us, event | category | flops | bytes accessed | tf_op | source)
XLA Modules:
  0.0 273.5 jit_solution(13897375159172938435)
XLA Ops:
  7.2 0.8 convert_reduce_fusion.3
  8.0 0.8 convolution_convert_fusion
  8.9 13.2 %all-reduce = (bf16[128,128]{1,0:T(8,128)(2,1)S(1)}, bf16[128]{0:T(256)(128)(2,1)S(1)}) all-reduce(bf16[128,128]{1,0:T(8,128)(2,1)S(1)} %convolution_convert_fusion, bf16[128]{0:T(256)(128)(2,1)S(1)} %convert_reduce_fusion.3), channel_id=1, replica_groups=mesh['parts'=2,'row'=4,'col'=4] {'col'}, use_global_device_ids=true, to_apply=%region_0.0 | all-reduce | flops 16512 | bytes 66048 | tf_op jit(solution)/shard_map/psum | solution.py:57
  22.1 1.0 convolution_divide_fusion
  23.0 1.8 add_convert_fusion
  24.9 3.5 %convert_reduce_fusion = f32[128,128]{1,0:T(8,128)S(1)} fusion(bf16[128,128,128]{2,1,0:T(8,128)(2,1)} %param.11), kind=kLoop, calls=%fused_computation.1 | loop fusion | flops 4177920 | bytes 4259840 | tf_op jit(solution)/shard_map/reduce_sum | solution.py:27
  28.4 4.8 %fusion.2 = f32[128,128]{1,0:T(8,128)S(1)} fusion(bf16[128,128,128]{2,1,0:T(8,128)(2,1)S(1)} %copy-done.3, f32[128,128]{1,0:T(8,128)S(1)} %broadcast_multiply_fusion), kind=kLoop, calls=%fused_computation.4 | loop fusion | flops 8372224 | bytes 4325376 | tf_op jit(solution)/shard_map/reduce_sum | solution.py:29
  33.2 11.7 %all-gather.11.cloned.1.call-done = bf16[8,128,768]{1,2,0:T(8,128)(2,1)} async-done(((bf16[8,128,192]{1,2,0:T(8,128)(2,1)}), bf16[8,128,768]{1,2,0:T(8,128)(2,1)}) %all-gather.11.cloned.1.call-update) | async-done | bytes 1572880 | tf_op jit(solution)/shard_map/all_gather | solution.py:73
  45.0 1.7 convert_reduce_fusion.2
  46.7 1.8 fusion.25
  48.6 3.2 %fusion.85 = (bf16[4,8,128,192]{2,3,0,1:T(8,128)(2,1)S(1)}, f32[4,8,128,192]{2,3,0,1:T(8,128)}) fusion(bf16[2,4,192,768]{3,2,1,0:T(8,128)(2,1)S(1)} %copy-done.12, bf16[8,128,768]{1,2,0:T(8,128)(2,1)S(1)} %copy-done.5, f32[8,128]{1,0:T(8,128)S(1)} %add_rsqrt_fusion.2, f32[8,128]{1,0:T(8,128)S(1)} %broadcast_multiply_fusion.2), kind=kOutput, calls=%fused_computation.115 | convolution fusion | flops 1211891712 | bytes 7479296 | tf_op jit(solution)/shard_map/std,fed->fste/dot_general | solution.py:75
  51.8 1.0 slice_bitcast_fusion.3
  52.7 1.5 collective-permute-start
  54.2 6.0 %fusion.38 = bf16[2,16,128,128]{3,1,0,2:T(8,128)(2,1)S(1)} fusion(bf16[128,128,128]{2,1,0:T(8,128)(2,1)S(1)} %copy-done.4, f32[128,128]{1,0:T(8,128)S(1)} %add_rsqrt_fusion, f32[128,128]{1,0:T(8,128)S(1)} %broadcast_multiply_fusion, bf16[128,2,16]{0,2,1:T(8,128)(2,1)S(1)} %copy-done.13), kind=kOutput, calls=%fused_computation.43 | convolution fusion | flops 143130624 | bytes 5382144 | tf_op jit(solution)/shard_map/ijc,clh->lhij/dot_general | solution.py:66
  60.2 0.2 slice_bitcast_fusion
  60.4 0.9 copy.26
  61.4 3.5 %all-to-all-start = ((bf16[16,128,128]{2,1,0:T(8,128)(2,1)}), bf16[16,128,128]{2,1,0:T(8,128)(2,1)S(1)}, u32[]{:S(2)}, u32[]{:S(2)}) async-start(bf16[16,128,128]{2,1,0:T(8,128)(2,1)} %copy.26), calls=%async_computation | async-start | bytes 1048576 | tf_op jit(solution)/shard_map/all_to_all | solution.py:72
  64.9 0.9 collective-permute-done
  65.8 0.6 collective-permute-start.1
  66.4 14.7 %all-gather.3 = bf16[4,1,128]{2,1,0:T(2,128)(2,1)S(1)} all-gather(bf16[1,1,128]{2,1,0:T(2,128)(2,1)S(1)} %fusion.80), channel_id=2, replica_groups=mesh['parts'=2,'row'=4,'col'=4] {'row'}, dimensions={0}, use_global_device_ids=true | all-gather | bytes 1280 | tf_op jit(solution)/shard_map/all_gather | solution.py:120
  81.3 0.1 copy_bitcast_fusion.1
  81.5 0.9 collective-permute-start.2
  82.3 0.1 broadcast.111.clone
  82.5 1.1 constant_dynamic-update-slice_fusion.7
  83.6 0.1 constant_dynamic-update-slice_fusion.6
  83.7 0.1 constant_dynamic-update-slice_fusion.5
  83.8 11.1 %collective-permute-done.2 = bf16[8,128,192]{1,2,0:T(8,128)(2,1)S(1)} collective-permute-done((bf16[8,128,192]{1,2,0:T(8,128)(2,1)S(1)}, bf16[8,128,192]{1,2,0:T(8,128)(2,1)S(1)}, u32[]{:S(2)}, u32[]{:S(2)}) %collective-permute-start.2) | collective-permute-done | bytes 393248 | tf_op jit(solution)/shard_map/ppermute | solution.py:21
  94.9 0.1 constant_dynamic-update-slice_fusion.4
  95.0 1.9 fusion.8
  96.9 3.2 %copy-done.2 = f32[8,4,128,512]{3,2,1,0:T(8,128)} copy-done((f32[8,4,128,512]{3,2,1,0:T(8,128)}, f32[8,4,128,512]{3,2,1,0:T(8,128)S(1)}, u32[]{:S(2)}) %copy-start.2) | copy-done | bytes 8388632
  100.1 2.3 fusion.4
  102.5 16.1 %all-gather.19.cloned.1.call-done = bf16[1,8,512,192]{2,3,0,1:T(8,128)(2,1)} async-done(((bf16[1,8,128,192]{2,3,0,1:T(8,128)(2,1)}), bf16[1,8,512,192]{2,3,0,1:T(8,128)(2,1)}) %all-gather.19.cloned.1.call-update) | async-done | bytes 1572880 | tf_op jit(solution)/shard_map/all_gather | solution.py:119
  118.5 6.3 %fusion.56 = f32[8,128,4,48]{1,3,2,0:T(8,128)S(1)} fusion(bf16[8,512,4,48]{1,3,2,0:T(8,128)(2,1)} %bitcast.146, f32[8,4,128,512]{3,2,1,0:T(8,128)} %copy-done.2, f32[8,4,128]{2,1,0:T(4,128)S(1)} %broadcast_maximum_fusion.1, f32[4,128,512]{2,1,0:T(8,128)S(1)} %copy_bitcast_fusion.1, pred[512]{0:T(512)(128)(4,1)S(1)} %bitcast.142, f32[8,128,4]{1,2,0:T(4,128)S(1)} %bitcast.139), kind=kOutput, calls=%fused_computation.61 | convolution fusion | flops 212008960 | bytes 11829760 | tf_op jit(solution)/shard_map/shqk,skhd->shqd/dot_general | solution.py:105
  124.9 2.1 fusion.69
  127.0 0.0 all-gather.15.cloned.1.call-start
  127.1 18.2 %all-gather.13.cloned.1.call-done = bf16[8,128,768]{1,2,0:T(8,128)(2,1)} async-done(((bf16[8,128,192]{1,2,0:T(8,128)(2,1)}), bf16[8,128,768]{1,2,0:T(8,128)(2,1)}) %all-gather.13.cloned.1.call-update) | async-done | bytes 1572880 | tf_op jit(solution)/shard_map/all_gather | solution.py:134
  145.2 2.6 fusion.47
  147.9 19.8 %all-gather.15.cloned.1.call-done = bf16[8,128,768]{1,2,0:T(8,128)(2,1)} async-done(((bf16[8,128,192]{1,2,0:T(8,128)(2,1)}), bf16[8,128,768]{1,2,0:T(8,128)(2,1)}) %all-gather.15.cloned.1.call-update) | async-done | bytes 1572880 | tf_op jit(solution)/shard_map/all_gather | solution.py:73
  167.7 1.7 convert_reduce_fusion.1
  169.4 1.8 fusion.23
  171.3 4.4 %fusion.86 = (bf16[4,8,128,192]{2,3,0,1:T(8,128)(2,1)S(1)}, f32[4,8,128,192]{2,3,0,1:T(8,128)}) fusion(bf16[2,4,192,768]{3,2,1,0:T(8,128)(2,1)} %param.18, bf16[8,128,768]{1,2,0:T(8,128)(2,1)S(1)} %copy-done.6, f32[8,128]{1,0:T(8,128)S(1)} %add_rsqrt_fusion.1, f32[8,128]{1,0:T(8,128)S(1)} %broadcast_multiply_fusion.1), kind=kOutput, calls=%fused_computation.116 | convolution fusion | flops 1211891712 | bytes 7479296 | tf_op jit(solution)/shard_map/std,fed->fste/dot_general | solution.py:75
  175.7 1.2 copy-done.10
  176.9 0.8 slice_bitcast_fusion.2
  177.8 1.5 collective-permute-start.3
  179.2 0.9 copy.29
  180.2 3.5 %all-to-all-start.1 = ((bf16[16,128,128]{2,1,0:T(8,128)(2,1)}), bf16[16,128,128]{2,1,0:T(8,128)(2,1)S(1)}, u32[]{:S(2)}, u32[]{:S(2)}) async-start(bf16[16,128,128]{2,1,0:T(8,128)(2,1)} %copy.29), calls=%async_computation.1 | async-start | bytes 1048576 | tf_op jit(solution)/shard_map/all_to_all | solution.py:72
  183.7 7.1 %collective-permute-done.3 = bf16[8,128,192]{1,2,0:T(8,128)(2,1)S(1)} collective-permute-done((bf16[8,128,192]{1,2,0:T(8,128)(2,1)S(1)}, bf16[8,128,192]{1,2,0:T(8,128)(2,1)S(1)}, u32[]{:S(2)}, u32[]{:S(2)}) %collective-permute-start.3) | collective-permute-done | bytes 393248 | tf_op jit(solution)/shard_map/ppermute | solution.py:21
  190.9 1.6 all-to-all-done.1
  192.4 0.1 copy_bitcast_fusion
  192.6 10.5 %collective-permute-done.4 = bf16[8,128,192]{1,2,0:T(8,128)(2,1)S(1)} collective-permute-done((bf16[8,128,192]{1,2,0:T(8,128)(2,1)S(1)}, bf16[8,128,192]{1,2,0:T(8,128)(2,1)S(1)}, u32[]{:S(2)}, u32[]{:S(2)}) %collective-permute-start.4) | collective-permute-done | bytes 393248 | tf_op jit(solution)/shard_map/ppermute | solution.py:21
  203.1 0.1 broadcast.111
  203.2 1.1 constant_dynamic-update-slice_fusion.3
  204.4 0.1 constant_dynamic-update-slice_fusion.2
  204.5 0.1 constant_dynamic-update-slice_fusion.1
  204.6 19.9 %collective-permute-done.5 = bf16[8,128,192]{1,2,0:T(8,128)(2,1)S(1)} collective-permute-done((bf16[8,128,192]{1,2,0:T(8,128)(2,1)S(1)}, bf16[8,128,192]{1,2,0:T(8,128)(2,1)S(1)}, u32[]{:S(2)}, u32[]{:S(2)}) %collective-permute-start.5) | collective-permute-done | bytes 393248 | tf_op jit(solution)/shard_map/ppermute | solution.py:21
  224.5 0.1 constant_dynamic-update-slice_fusion
  224.6 1.9 fusion.9
  226.5 3.2 %copy-done.1 = f32[8,4,128,512]{3,2,1,0:T(8,128)} copy-done((f32[8,4,128,512]{3,2,1,0:T(8,128)}, f32[8,4,128,512]{3,2,1,0:T(8,128)S(1)}, u32[]{:S(2)}) %copy-start.1) | copy-done | bytes 8388632
  229.7 2.3 fusion.6
  232.1 5.5 %all-gather.21.cloned.1.call-done = bf16[1,8,512,192]{2,3,0,1:T(8,128)(2,1)} async-done(((bf16[1,8,128,192]{2,3,0,1:T(8,128)(2,1)}), bf16[1,8,512,192]{2,3,0,1:T(8,128)(2,1)}) %all-gather.21.cloned.1.call-update) | async-done | bytes 1572880 | tf_op jit(solution)/shard_map/all_gather | solution.py:119
  237.6 6.3 %fusion.53 = f32[8,128,4,48]{1,3,2,0:T(8,128)S(1)} fusion(bf16[8,512,4,48]{1,3,2,0:T(8,128)(2,1)} %bitcast.147, f32[8,4,128,512]{3,2,1,0:T(8,128)} %copy-done.1, f32[8,4,128]{2,1,0:T(4,128)S(1)} %broadcast_maximum_fusion, f32[4,128,512]{2,1,0:T(8,128)S(1)} %copy_bitcast_fusion, pred[512]{0:T(512)(128)(4,1)S(1)} %bitcast.145, f32[8,128,4]{1,2,0:T(4,128)S(1)} %bitcast.138), kind=kOutput, calls=%fused_computation.60 | convolution fusion | flops 212008960 | bytes 11829760 | tf_op jit(solution)/shard_map/shqk,skhd->shqd/dot_general | solution.py:105
  243.9 2.1 fusion.70
  246.0 18.0 %all-gather.17.cloned.1.call-done = bf16[8,128,768]{1,2,0:T(8,128)(2,1)} async-done(((bf16[8,128,192]{1,2,0:T(8,128)(2,1)}), bf16[8,128,768]{1,2,0:T(8,128)(2,1)}) %all-gather.17.cloned.1.call-update) | async-done | bytes 1572880 | tf_op jit(solution)/shard_map/all_gather | solution.py:134
  264.0 2.6 fusion.48
  (54 shorter events, 0.4 us)
Async XLA Ops:
  6.5 1.5 copy-start
  6.5 38.4 %all-gather.11.cloned.1.call-start = ((), (), s32[]{:S(2)}) async-start(), calls=%async_computation.2 | async-start | bytes 1966080 | tf_op jit(solution)/shard_map/all_gather | solution.py:73
  24.9 3.5 %copy-start.3 = (bf16[128,128,128]{2,1,0:T(8,128)(2,1)S(1)}, bf16[128,128,128]{2,1,0:T(8,128)(2,1)}, u32[]{:S(2)}) copy-start(bf16[128,128,128]{2,1,0:T(8,128)(2,1)} %param.11) | copy-start | bytes 12582916
  28.4 20.2 %copy-start.12 = (bf16[2,4,192,768]{3,2,1,0:T(8,128)(2,1)S(1)}, bf16[2,4,192,768]{3,2,1,0:T(8,128)(2,1)}, u32[]{:S(2)}) copy-start(bf16[2,4,192,768]{3,2,1,0:T(8,128)(2,1)} %param.18) | copy-start | bytes 7077892
  45.0 3.6 %copy-start.5 = (bf16[8,128,768]{1,2,0:T(8,128)(2,1)S(1)}, bf16[8,128,768]{1,2,0:T(8,128)(2,1)}, u32[]{:S(2)}) copy-start(bf16[8,128,768]{1,2,0:T(8,128)(2,1)} %all-gather.11.cloned.1.call-done) | copy-start | bytes 4718596
  48.6 5.6 %copy-start.4 = (bf16[128,128,128]{2,1,0:T(8,128)(2,1)S(1)}, bf16[128,128,128]{2,1,0:T(8,128)(2,1)}, u32[]{:S(2)}) copy-start(bf16[128,128,128]{2,1,0:T(8,128)(2,1)} %param.11) | copy-start | bytes 12582916
  48.6 5.6 %copy-start.13 = (bf16[128,2,16]{0,2,1:T(8,128)(2,1)S(1)}, bf16[128,2,16]{0,2,1:T(8,128)(2,1)}, u32[]{:S(2)}) copy-start(bf16[128,2,16]{0,2,1:T(8,128)(2,1)} %param.17) | copy-start | bytes 24580
  51.8 8.4 %copy-start.9 = (bf16[4,8,128,192]{2,3,0,1:T(8,128)(2,1)}, bf16[4,8,128,192]{2,3,0,1:T(8,128)(2,1)S(1)}, u32[]{:S(2)}) copy-start(bf16[4,8,128,192]{2,3,0,1:T(8,128)(2,1)S(1)} %get-tuple-element.15) | copy-start | bytes 4718596
  52.7 13.0 %collective-permute-start = (bf16[8,128,192]{1,2,0:T(8,128)(2,1)S(1)}, bf16[8,128,192]{1,2,0:T(8,128)(2,1)S(1)}, u32[]{:S(2)}, u32[]{:S(2)}) collective-permute-start(bf16[8,128,192]{1,2,0:T(8,128)(2,1)S(1)} %get-tuple-element.10), channel_id=1, source_target_pairs={{0,4},{4,8},{8,12},{12,0},{1,5},{5,9},{9,13},{13,1},{2,6},{6,10},{... | collective-permute-start | bytes 1179656 | tf_op jit(solution)/shard_map/ppermute | solution.py:21
  60.2 6.2 %copy-start.14 = (s32[128]{0:T(128)S(1)}, s32[128]{0:T(128)}, u32[]{:S(2)}) copy-start(s32[128]{0:T(128)} %param.12) | copy-start | bytes 1540
  61.4 20.0 %all-to-all-start = ((bf16[16,128,128]{2,1,0:T(8,128)(2,1)}), bf16[16,128,128]{2,1,0:T(8,128)(2,1)S(1)}, u32[]{:S(2)}, u32[]{:S(2)}) async-start(bf16[16,128,128]{2,1,0:T(8,128)(2,1)} %copy.26), calls=%async_computation | async-start | bytes 1048576 | tf_op jit(solution)/shard_map/all_to_all | solution.py:72
  64.8 53.7 %all-gather.19.cloned.1.call-start = ((), (), s32[]{:S(2)}) async-start(), calls=%async_computation.6 | async-start | bytes 1966080 | tf_op jit(solution)/shard_map/all_gather | solution.py:119
  65.8 15.7 %collective-permute-start.1 = (bf16[8,128,192]{1,2,0:T(8,128)(2,1)S(1)}, bf16[8,128,192]{1,2,0:T(8,128)(2,1)S(1)}, u32[]{:S(2)}, u32[]{:S(2)}) collective-permute-start(bf16[8,128,192]{1,2,0:T(8,128)(2,1)S(1)} %collective-permute-done), channel_id=1, source_target_pairs={{0,4},{4,8},{8,12},{12,0},{1,5},{5,9},{9,13},{13,1},{2,6},{6,10},{... | collective-permute-start | bytes 1179656 | tf_op jit(solution)/shard_map/ppermute | solution.py:21
  81.2 64.0 %all-gather.13.cloned.1.call-start = ((), (), s32[]{:S(2)}) async-start(), calls=%async_computation.3 | async-start | bytes 1966080 | tf_op jit(solution)/shard_map/all_gather | solution.py:134
  81.5 13.4 %collective-permute-start.2 = (bf16[8,128,192]{1,2,0:T(8,128)(2,1)S(1)}, bf16[8,128,192]{1,2,0:T(8,128)(2,1)S(1)}, u32[]{:S(2)}, u32[]{:S(2)}) collective-permute-start(bf16[8,128,192]{1,2,0:T(8,128)(2,1)S(1)} %collective-permute-done.1), channel_id=1, source_target_pairs={{0,4},{4,8},{8,12},{12,0},{1,5},{5,9},{9,13},{13,1},{2,6},{6,10},{... | collective-permute-start | bytes 1179656 | tf_op jit(solution)/shard_map/ppermute | solution.py:21
  96.9 3.2 %copy-start.2 = (f32[8,4,128,512]{3,2,1,0:T(8,128)}, f32[8,4,128,512]{3,2,1,0:T(8,128)S(1)}, u32[]{:S(2)}) copy-start(f32[8,4,128,512]{3,2,1,0:T(8,128)S(1)} %get-tuple-element.18) | copy-start | bytes 25165828
  118.5 26.7 %copy-start.7 = (bf16[8,128,192]{1,2,0:T(8,128)(2,1)S(1)}, bf16[8,128,192]{1,2,0:T(8,128)(2,1)}, u32[]{:S(2)}) copy-start(bf16[8,128,192]{1,2,0:T(8,128)(2,1)} %add_convert_fusion) | copy-start | bytes 1179652
  118.5 26.7 %copy-start.11 = (bf16[2,192,768]{2,1,0:T(8,128)(2,1)S(1)}, bf16[2,192,768]{2,1,0:T(8,128)(2,1)}, u32[]{:S(2)}) copy-start(bf16[2,192,768]{2,1,0:T(8,128)(2,1)} %param.19) | copy-start | bytes 1769476
  127.0 40.7 %all-gather.15.cloned.1.call-start = ((), (), s32[]{:S(2)}) async-start(), calls=%async_computation.4 | async-start | bytes 1966080 | tf_op jit(solution)/shard_map/all_gather | solution.py:73
  167.7 3.6 %copy-start.6 = (bf16[8,128,768]{1,2,0:T(8,128)(2,1)S(1)}, bf16[8,128,768]{1,2,0:T(8,128)(2,1)}, u32[]{:S(2)}) copy-start(bf16[8,128,768]{1,2,0:T(8,128)(2,1)} %all-gather.15.cloned.1.call-done) | copy-start | bytes 4718596
  175.7 1.2 copy-start.10
  177.8 13.0 %collective-permute-start.3 = (bf16[8,128,192]{1,2,0:T(8,128)(2,1)S(1)}, bf16[8,128,192]{1,2,0:T(8,128)(2,1)S(1)}, u32[]{:S(2)}, u32[]{:S(2)}) collective-permute-start(bf16[8,128,192]{1,2,0:T(8,128)(2,1)S(1)} %get-tuple-element.7), channel_id=1, source_target_pairs={{0,4},{4,8},{8,12},{12,0},{1,5},{5,9},{9,13},{13,1},{2,6},{6,10},{... | collective-permute-start | bytes 1179656 | tf_op jit(solution)/shard_map/ppermute | solution.py:21
  180.2 12.3 %all-to-all-start.1 = ((bf16[16,128,128]{2,1,0:T(8,128)(2,1)}), bf16[16,128,128]{2,1,0:T(8,128)(2,1)S(1)}, u32[]{:S(2)}, u32[]{:S(2)}) async-start(bf16[16,128,128]{2,1,0:T(8,128)(2,1)} %copy.29), calls=%async_computation.1 | async-start | bytes 1048576 | tf_op jit(solution)/shard_map/all_to_all | solution.py:72
  183.7 53.9 %all-gather.21.cloned.1.call-start = ((), (), s32[]{:S(2)}) async-start(), calls=%async_computation.7 | async-start | bytes 1966080 | tf_op jit(solution)/shard_map/all_gather | solution.py:119
  190.8 12.3 %collective-permute-start.4 = (bf16[8,128,192]{1,2,0:T(8,128)(2,1)S(1)}, bf16[8,128,192]{1,2,0:T(8,128)(2,1)S(1)}, u32[]{:S(2)}, u32[]{:S(2)}) collective-permute-start(bf16[8,128,192]{1,2,0:T(8,128)(2,1)S(1)} %collective-permute-done.3), channel_id=1, source_target_pairs={{0,4},{4,8},{8,12},{12,0},{1,5},{5,9},{9,13},{13,1},{2,6},{6,10},{... | collective-permute-start | bytes 1179656 | tf_op jit(solution)/shard_map/ppermute | solution.py:21
  190.8 73.2 %all-gather.17.cloned.1.call-start = ((), (), s32[]{:S(2)}) async-start(), calls=%async_computation.5 | async-start | bytes 1966080 | tf_op jit(solution)/shard_map/all_gather | solution.py:134
  203.1 21.4 %collective-permute-start.5 = (bf16[8,128,192]{1,2,0:T(8,128)(2,1)S(1)}, bf16[8,128,192]{1,2,0:T(8,128)(2,1)S(1)}, u32[]{:S(2)}, u32[]{:S(2)}) collective-permute-start(bf16[8,128,192]{1,2,0:T(8,128)(2,1)S(1)} %collective-permute-done.4), channel_id=1, source_target_pairs={{0,4},{4,8},{8,12},{12,0},{1,5},{5,9},{9,13},{13,1},{2,6},{6,10},{... | collective-permute-start | bytes 1179656 | tf_op jit(solution)/shard_map/ppermute | solution.py:21
  226.5 3.2 %copy-start.1 = (f32[8,4,128,512]{3,2,1,0:T(8,128)}, f32[8,4,128,512]{3,2,1,0:T(8,128)S(1)}, u32[]{:S(2)}) copy-start(f32[8,4,128,512]{3,2,1,0:T(8,128)S(1)} %get-tuple-element.22) | copy-start | bytes 25165828
  237.6 26.4 %copy-start.8 = (bf16[8,128,192]{1,2,0:T(8,128)(2,1)S(1)}, bf16[8,128,192]{1,2,0:T(8,128)(2,1)}, u32[]{:S(2)}) copy-start(bf16[8,128,192]{1,2,0:T(8,128)(2,1)} %fusion.47) | copy-start | bytes 1179652
Sparse Core Ops, SparseCore 0:
  25.0 19.9 all-gather.10
  81.3 37.1 all-gather.18
  127.1 18.0 all-gather.12
  148.0 19.6 all-gather.14
  191.0 46.5 all-gather.20
  246.2 17.8 all-gather.16
